TPU v7x, 32 devices: a whole 2x2x4 slice. The times are simulated.
32 devices in a mesh: rows: 8 (over z, y), grp: 4 (over x, core).
Axes of the slice: x: 2, y: 2, z: 4, core: 2. Of those that a mesh axis runs over, the one named last changes fastest.
Arguments:
- embeddings: float32 [4096, 768], P(('rows', 'grp')), may hold values from -100 to 100
- assignments: int32 [4096], P(('rows', 'grp')), may hold values from 0 to 16383, as said below
Outputs:
- whitened: float32 [4096, 768], P(('rows', 'grp'))
- centroid_means: float32 [16384, 768], P(('rows', 'grp'))
Inputs may be any that keep to these rules, and one draw needn't show every extreme that they name: `assignments`: owner o holds the 2048 centroids o * 2048 to (o + 1) * 2048 - 1. The 128 rows of one device name centroids of at most 32 rows for any one owner, and exactly 32 for some owner. Some centroids are named by no row.
All inputs are finite; a program needn't handle non-finite values.
Results may differ from a plain program's by a relative error of at most 0.00007.
Values sent between devices are 32-bit elements; how exact they have to be, the bound alone decides.
A program may use at most 64 MiB of HBM per device.

v0:
```python
import jax
import jax.numpy as jnp
from jax import lax
from jax.sharding import PartitionSpec as P

CENTROIDS = 16384


def whiten_rows(factor, values):
    return lax.linalg.triangular_solve(
        factor, values, left_side=False, lower=True, transpose_a=True
    )


def body(embeddings, assignments):
    rows_here = embeddings.shape[0]
    width = embeddings.shape[1]
    owners = lax.axis_size("rows")
    groups = lax.axis_size("grp")
    total = rows_here * owners * groups
    partial_value = jnp.dot(
        embeddings.T,
        embeddings,
        precision=lax.Precision.HIGHEST,
        preferred_element_type=jnp.float32,
    )
    gram = lax.psum(partial_value, ("rows", "grp"))
    factor = jnp.linalg.cholesky(gram / total + 1e-05 * jnp.eye(width, dtype=jnp.float32))
    whitened = whiten_rows(factor, embeddings)
    per_owner = CENTROIDS // owners
    capacity = max(2, 2 * rows_here // owners)
    target = assignments // per_owner
    local = assignments % per_owner
    hits = (target[:, None] == jnp.arange(owners, dtype=jnp.int32)[None, :]).astype(jnp.int32)
    rank = jnp.sum(hits * (jnp.cumsum(hits, axis=0) - 1), axis=1)
    slot = target * capacity + rank
    outgoing = jnp.zeros((owners * capacity, width), jnp.float32).at[slot].set(embeddings)
    labels = jnp.full((owners * capacity,), -1, jnp.int32).at[slot].set(local)
    incoming, tags = (
        lax.all_to_all(
            outgoing.reshape(owners, capacity, width),
            "rows",
            split_axis=0,
            concat_axis=0,
            tiled=True,
        ),
        lax.all_to_all(
            labels.reshape(owners, capacity), "rows", split_axis=0, concat_axis=0, tiled=True
        ),
    )
    member = (tags.reshape(-1)[None, :] == jnp.arange(per_owner, dtype=jnp.int32)[:, None]).astype(
        jnp.float32
    )
    list_sums = jnp.dot(
        member,
        incoming.reshape(-1, width),
        precision=lax.Precision.HIGHEST,
        preferred_element_type=jnp.float32,
    )
    list_counts = jnp.sum(member, axis=1)
    list_sums, list_counts = (
        lax.psum_scatter(list_sums, "grp", scatter_dimension=0, tiled=True),
        lax.psum_scatter(list_counts, "grp", scatter_dimension=0, tiled=True),
    )
    list_sums = whiten_rows(factor, list_sums)
    centroid_means = list_sums / jnp.maximum(list_counts, 1.0)[:, None]
    return (whitened, centroid_means)


def solution(mesh):
    return jax.shard_map(
        body,
        mesh=mesh,
        in_specs=(P(("rows", "grp"), None), P(("rows", "grp"))),
        out_specs=(P(("rows", "grp"), None), P(("rows", "grp"), None)),
        check_vma=False,
    )
```

profile of v0, /device:TPU:0, one launch (start us, length us, event | category | flops | bytes accessed | tf_op | source)
XLA Modules:
  0.0 455.5 jit_solution(11934431538999040726)
XLA Ops:
  10.8 7.3 %all-to-all-start = ((s32[8,1,32]{2,1,0:T(1,128)}), s32[8,1,32]{2,1,0:T(1,128)S(1)}, u32[]{:S(2)}, u32[]{:S(2)}) async-start(s32[8,1,32]{2,1,0:T(1,128)} %all_to_all.9), calls=%async_computation | async-start | bytes 8192 | tf_op jit(solution)/shard_map/all_to_all | solution.py:47
  18.1 2.4 scatter_custom_fusion.1
  20.5 4.1 all-to-all-done
  24.6 3.5 all-to-all-start.1
  28.2 3.5 fusion.86
  33.0 16.6 %all-to-all-done.1 = f32[8,32,768]{2,1,0:T(8,128)S(1)} async-done(((f32[8,32,768]{2,1,0:T(8,128)}), f32[8,32,768]{2,1,0:T(8,128)S(1)}, u32[]{:S(2)}, u32[]{:S(2)}) %all-to-all-start.1) | async-done | bytes 786464 | tf_op jit(solution)/shard_map/all_to_all | solution.py:40
  49.6 4.7 %fusion.1 = f32[2048,768]{1,0:T(8,128)} fusion(f32[256,768]{1,0:T(8,128)S(1)} %bitcast.107, s32[256]{0:T(256)S(1)} %eq.37), kind=kOutput, calls=%fused_computation.12 | convolution fusion | flops 4832362496 | bytes 7078912 | tf_op jit(solution)/shard_map/dot_general | solution.py:54
  56.6 5.9 %all-reduce.1 = f32[2048]{0:T(1024)S(1)} all-reduce(f32[2048]{0:T(1024)S(1)} %convert_reduce_fusion), channel_id=3, replica_groups=mesh['rows'=8,'grp'=4] {'grp'}, use_global_device_ids=true, to_apply=%region_19.20.clone | all-reduce | flops 2048 | bytes 16384
  62.6 127.0 %all-reduce.4.cloned.1.call-done = f32[768,768]{0,1:T(8,128)} async-done(((f32[768,768]{0,1:T(8,128)}), f32[768,768]{0,1:T(8,128)}) %all-reduce.4.cloned.1.call-update) | async-done | bytes 2359312 | tf_op jit(solution)/shard_map/psum | solution.py:27
  189.6 3.3 select_add_fusion
  193.0 3.5 copy.53
  199.9 11.7 %cholesky.164 = f32[128,128]{1,0:T(8,128)S(1)} custom-call(f32[128,128]{1,0:T(8,128)S(1)} %cholesky.421), custom_call_target="Cholesky" | custom-call | tf_op jit(solution)/shard_map/jit(cholesky)/cholesky | solution.py:28
  212.3 9.8 %custom-call.48 = f32[1,128,128]{1,2,0:T(8,128)S(1)} custom-call(f32[1,128,128]{2,1,0:T(8,128)S(1)} %get-tuple-element.73), custom_call_target="InvertDiagBlocksLowerTriangular" | custom-call | tf_op jit(solution)/shard_map/jit(cholesky)/cholesky | solution.py:28
  225.1 11.7 %cholesky.187 = f32[128,128]{1,0:T(8,128)S(1)} custom-call(f32[128,128]{1,0:T(8,128)S(1)} %cholesky.425), custom_call_target="Cholesky" | custom-call | tf_op jit(solution)/shard_map/jit(cholesky)/cholesky | solution.py:28
  238.6 11.1 %custom-call.49 = f32[1,128,128]{1,2,0:T(8,128)S(1)} custom-call(f32[1,128,128]{2,1,0:T(8,128)} %get-tuple-element.71), custom_call_target="InvertDiagBlocksLowerTriangular" | custom-call | tf_op jit(solution)/shard_map/jit(cholesky)/cholesky | solution.py:28
  252.1 11.7 %cholesky.352 = f32[128,128]{1,0:T(8,128)S(1)} custom-call(f32[128,128]{1,0:T(8,128)S(1)} %cholesky.430), custom_call_target="Cholesky" | custom-call | tf_op jit(solution)/shard_map/jit(cholesky)/cholesky | solution.py:28
  264.0 9.8 %custom-call.50 = f32[1,128,128]{1,2,0:T(8,128)S(1)} custom-call(f32[1,128,128]{2,1,0:T(8,128)S(1)} %get-tuple-element.69), custom_call_target="InvertDiagBlocksLowerTriangular" | custom-call | tf_op jit(solution)/shard_map/jit(cholesky)/cholesky | solution.py:28
  274.2 2.1 convolution_subtract_fusion.7
  276.3 11.9 %cholesky.371 = f32[128,128]{1,0:T(8,128)S(1)} custom-call(f32[128,128]{1,0:T(8,128)S(1)} %cholesky.435), custom_call_target="Cholesky" | custom-call | tf_op jit(solution)/shard_map/jit(cholesky)/cholesky | solution.py:28
  288.3 9.8 %custom-call.51 = f32[1,128,128]{1,2,0:T(8,128)S(1)} custom-call(f32[1,128,128]{2,1,0:T(8,128)S(1)} %get-tuple-element.67), custom_call_target="InvertDiagBlocksLowerTriangular" | custom-call | tf_op jit(solution)/shard_map/jit(cholesky)/cholesky | solution.py:28
  300.4 11.7 %cholesky.390 = f32[128,128]{1,0:T(8,128)S(1)} custom-call(f32[128,128]{1,0:T(8,128)S(1)} %cholesky.440), custom_call_target="Cholesky" | custom-call | tf_op jit(solution)/shard_map/jit(cholesky)/cholesky | solution.py:28
  312.2 9.8 %custom-call.52 = f32[1,128,128]{1,2,0:T(8,128)S(1)} custom-call(f32[1,128,128]{2,1,0:T(8,128)S(1)} %get-tuple-element.65), custom_call_target="InvertDiagBlocksLowerTriangular" | custom-call | tf_op jit(solution)/shard_map/jit(cholesky)/cholesky | solution.py:28
  323.9 11.7 %cholesky.408 = f32[128,128]{1,0:T(8,128)S(1)} custom-call(f32[128,128]{1,0:T(8,128)S(1)} %convolution_subtract_fusion.12), custom_call_target="Cholesky" | custom-call | tf_op jit(solution)/shard_map/jit(cholesky)/cholesky | solution.py:28
  344.4 21.6 %while.1 = (s32[]{:T(128)}, f32[768,768]{0,1:T(8,128)}, s32[6,2]{0,1:T(2,128)S(1)}, f32[6,128,128]{2,1,0:T(8,128)}, s32[]{:T(128)}) while((s32[]{:T(128)}, f32[768,768]{0,1:T(8,128)}, s32[6,2]{0,1:T(2,128)S(1)}, f32[6,128,128]{2,1,0:T(8,128)}, s32[]{:T(128)}) %tuple.56), condition=%wide.while_cond, body=%wide.while_body.sunk | while | flops 2 | bytes 393829 | solution.py:10
  345.0 2.3 dynamic-slice.10
  348.6 2.3 dynamic-slice.10
  352.2 2.3 dynamic-slice.10
  355.8 2.3 dynamic-slice.10
  359.4 2.3 dynamic-slice.10
  363.1 2.2 dynamic-slice.10
  366.0 60.1 %custom-call.53 = f32[6,128,128]{1,2,0:T(8,128)S(1)} custom-call(f32[6,128,128]{2,1,0:T(8,128)} %get-tuple-element.9), custom_call_target="InvertDiagBlocksLowerTriangular" | custom-call | tf_op jit(solution)/shard_map/triangular_solve | solution.py:10
  443.1 2.3 convolution_subtract_fusion.1
  (122 shorter events, 54.0 us)
Async XLA Ops:
  8.0 20.2 %copy-start.3 = (f32[128,768]{1,0:T(8,128)S(1)}, f32[128,768]{1,0:T(8,128)}, u32[]{:S(2)}) copy-start(f32[128,768]{1,0:T(8,128)} %param.2) | copy-start | bytes 1179652
  10.8 13.7 %all-to-all-start = ((s32[8,1,32]{2,1,0:T(1,128)}), s32[8,1,32]{2,1,0:T(1,128)S(1)}, u32[]{:S(2)}, u32[]{:S(2)}) async-start(s32[8,1,32]{2,1,0:T(1,128)} %all_to_all.9), calls=%async_computation | async-start | bytes 8192 | tf_op jit(solution)/shard_map/all_to_all | solution.py:47
  24.6 25.1 %all-to-all-start.1 = ((f32[8,32,768]{2,1,0:T(8,128)}), f32[8,32,768]{2,1,0:T(8,128)S(1)}, u32[]{:S(2)}, u32[]{:S(2)}) async-start(f32[8,32,768]{2,1,0:T(8,128)} %bitcast.18), calls=%async_computation.1 | async-start | bytes 1572864 | tf_op jit(solution)/shard_map/all_to_all | solution.py:40
  28.1 161.5 %all-reduce.4.cloned.1.call-start = ((), (), s32[]{:S(2)}) async-start(), calls=%async_computation.3 | async-start | bytes 4718592 | tf_op jit(solution)/shard_map/psum | solution.py:27
  31.7 402.3 %reduce-scatter.2.cloned.1.call-start = ((), (), s32[]{:S(2)}) async-start(), calls=%async_computation.4 | async-start | bytes 7864320 | tf_op jit(solution)/shard_map/reduce_scatter | solution.py:62
  54.4 0.7 copy-start.5
  193.0 3.5 copy-start
  198.4 1.4 copy-start.2
  366.0 65.2 %copy-start.1 = (f32[768,768]{0,1:T(8,128)S(1)}, f32[768,768]{0,1:T(8,128)}, u32[]{:S(2)}) copy-start(f32[768,768]{0,1:T(8,128)} %get-tuple-element.137) | copy-start | bytes 7077892
  434.0 3.5 copy-start.4
Sparse Core Ops, SparseCore 0:
  34.5 155.1 all-reduce.3
Sparse Core Ops, SparseCore 1:
  54.5 57.8 reduce-scatter.1
where the time goes:
time: 462 us; the launch traced here: 455 us
  other arithmetic  194 us (42%)
  waiting for transfers between devices  148 us (32%)
  matrix products  38.5 us (8%)
  local copies, waits for them, and re-layouts  37.2 us (8%)
  between operations  20.9 us (5%)
  starting transfers between devices  10.9 us (2%)
  blocking collectives  5.88 us (1%)
    psum x1, waiting for transfers between devices, body(): gram = lax.psum(partial_value, ('rows', 'grp'))  127 us
    another operation x22, other arithmetic, body(): jnp.linalg.cholesky(gram / total + 1e-05 * jnp.eye(width, dtype=jnp.float...  125 us
    another operation x3, other arithmetic, whiten_rows(): lax.linalg.triangular_solve(factor, values, left_side=False, lower=True,...  61.7 us
    another operation x30, local copies, waits for them, and re-layouts  21.5 us
    another operation x22, matrix products, whiten_rows(): lax.linalg.triangular_solve(factor, values, left_side=False, lower=True,...  18.6 us
    all_to_all x1, waiting for transfers between devices, body(): lax.all_to_all(outgoing.reshape(owners, capacity, width), 'rows', split_a...  16.6 us
    another operation x10, matrix products, body(): jnp.linalg.cholesky(gram / total + 1e-05 * jnp.eye(width, dtype=jnp.float...  11.7 us
  transfers between devices with their start and end apart: 4, of which 3 were waited for; matrix products, arithmetic and copies ran while one was open for 55% of the time, Pallas kernels for 0%

commit v1 on v0

--- a/solution.py
+++ b/solution.py
@@ -1,15 +1,123 @@
+import functools
+
 import jax
 import jax.numpy as jnp
 from jax import lax
+from jax.experimental import pallas as pl
+from jax.experimental.pallas import tpu as pltpu
 from jax.sharding import PartitionSpec as P
 
 CENTROIDS = 16384
+BLOCK = 128
+PANEL = 8
 
 
-def whiten_rows(factor, values):
-    return lax.linalg.triangular_solve(
-        factor, values, left_side=False, lower=True, transpose_a=True
+def split3(value):
+    high = value.astype(jnp.bfloat16).astype(jnp.float32)
+    rest = value - high
+    mid = rest.astype(jnp.bfloat16).astype(jnp.float32)
+    return high, mid, rest - mid
+
+
+def dot(a, b, dims):
+    return lax.dot_general(
+        a, b, (dims, ((), ())), precision=lax.Precision.HIGHEST, preferred_element_type=jnp.float32
     )
+
+
+def invert_block(d_ref, v_ref):
+    def step(p, carry):
+        row = pl.multiple_of(p * PANEL, PANEL)
+        rows = d_ref[pl.ds(row, PANEL), :]
+        left, right = rows[:, :BLOCK], rows[:, BLOCK:]
+        rolled = pltpu.roll(left, lax.rem(BLOCK - row, BLOCK), 1)
+        full = (PANEL, BLOCK)
+        a = {}
+        for j in range(PANEL):
+            column = jnp.broadcast_to(rolled[:, j : j + 1], full)
+            for i in range(j, PANEL):
+                a[i, j] = jnp.broadcast_to(column[i : i + 1, :], full)
+        u = [jnp.broadcast_to(left[i : i + 1, :], full) for i in range(PANEL)]
+        v = [jnp.broadcast_to(right[i : i + 1, :], full) for i in range(PANEL)]
+        for j in range(PANEL):
+            scale = lax.rsqrt(a[j, j])
+            u[j] = u[j] * scale
+            v[j] = v[j] * scale
+            for i in range(j + 1, PANEL):
+                a[i, j] = a[i, j] * scale
+            for i in range(j + 1, PANEL):
+                for k in range(j + 1, i + 1):
+                    a[i, k] = a[i, k] - a[i, j] * a[k, j]
+                u[i] = u[i] - a[i, j] * u[j]
+                v[i] = v[i] - a[i, j] * v[j]
+        sub = lax.broadcasted_iota(jnp.int32, full, 0)
+        up, vp = u[0], v[0]
+        for i in range(1, PANEL):
+            up = jnp.where(sub == i, u[i], up)
+            vp = jnp.where(sub == i, v[i], vp)
+        v_ref[pl.ds(row, PANEL), :] = vp
+        uh, um, ul = split3(up)
+        vh, vm, vl = split3(vp)
+        lhs = jnp.concatenate([uh, uh, um, uh, um, ul], axis=0).astype(jnp.bfloat16)
+        rhs = jnp.concatenate(
+            [
+                jnp.concatenate([uh, um, uh, ul, um, uh], axis=0),
+                jnp.concatenate([vh, vm, vh, vl, vm, vh], axis=0),
+            ],
+            axis=1,
+        ).astype(jnp.bfloat16)
+        d_ref[...] = d_ref[...] - lax.dot_general(
+            lhs, rhs, (((0,), (0,)), ((), ())), preferred_element_type=jnp.float32
+        )
+        return carry
+
+    lax.fori_loop(0, BLOCK // PANEL, step, 0)
+
+
+def factor_kernel(total, gram_ref, e_ref, s_ref, n_ref, w_ref, m_ref, a_ref, x_ref, d_ref, v_ref):
+    width = gram_ref.shape[0]
+    r = lax.broadcasted_iota(jnp.int32, (BLOCK, BLOCK), 0)
+    c = lax.broadcasted_iota(jnp.int32, (BLOCK, BLOCK), 1)
+    eye = jnp.where(r == c, 1.0, 0.0).astype(jnp.float32)
+    a_ref[...] = gram_ref[...] / total
+    x_ref[...] = jnp.zeros_like(x_ref)
+    for lo in range(0, width, BLOCK):
+        hi = lo + BLOCK
+        here = slice(lo, hi)
+        d_ref[:, :BLOCK] = a_ref[here, here] + 1e-05 * eye
+        d_ref[:, BLOCK:] = eye
+        invert_block(d_ref, v_ref)
+        inv = v_ref[...]
+        x_ref[here, here] = inv
+        if lo > 0:
+            x_ref[here, :lo] = dot(inv, x_ref[here, :lo], ((1,), (0,)))
+        if hi < width:
+            upper = dot(inv, a_ref[here, hi:], ((1,), (0,)))
+            a_ref[hi:, hi:] = a_ref[hi:, hi:] - dot(upper, upper, ((0,), (0,)))
+            x_ref[hi:, :hi] = x_ref[hi:, :hi] - dot(upper, x_ref[here, :hi], ((0,), (0,)))
+    w_ref[...] = dot(e_ref[...], x_ref[...], ((1,), (1,)))
+    m_ref[...] = dot(s_ref[...], x_ref[...], ((1,), (1,))) / jnp.maximum(n_ref[...], 1.0)
+
+
+def factor_and_solve(gram, embeddings, sums, counts, total):
+    width = gram.shape[0]
+    vmem = pl.BlockSpec(memory_space=pltpu.VMEM)
+    return pl.pallas_call(
+        functools.partial(factor_kernel, float(total)),
+        out_shape=(
+            jax.ShapeDtypeStruct(embeddings.shape, jnp.float32),
+            jax.ShapeDtypeStruct(sums.shape, jnp.float32),
+        ),
+        in_specs=[vmem] * 4,
+        out_specs=(vmem, vmem),
+        scratch_shapes=[
+            pltpu.VMEM((width, width), jnp.float32),
+            pltpu.VMEM((width, width), jnp.float32),
+            pltpu.VMEM((BLOCK, 2 * BLOCK), jnp.float32),
+            pltpu.VMEM((BLOCK, BLOCK), jnp.float32),
+        ],
+        compiler_params=pltpu.CompilerParams(vmem_limit_bytes=48 * 1024 * 1024),
+    )(gram, embeddings, sums, counts)
 
 
 def body(embeddings, assignments):
@@ -25,8 +133,6 @@
         preferred_element_type=jnp.float32,
     )
     gram = lax.psum(partial_value, ("rows", "grp"))
-    factor = jnp.linalg.cholesky(gram / total + 1e-05 * jnp.eye(width, dtype=jnp.float32))
-    whitened = whiten_rows(factor, embeddings)
     per_owner = CENTROIDS // owners
     capacity = max(2, 2 * rows_here // owners)
     target = assignments // per_owner
@@ -62,9 +168,7 @@
         lax.psum_scatter(list_sums, "grp", scatter_dimension=0, tiled=True),
         lax.psum_scatter(list_counts, "grp", scatter_dimension=0, tiled=True),
     )
-    list_sums = whiten_rows(factor, list_sums)
-    centroid_means = list_sums / jnp.maximum(list_counts, 1.0)[:, None]
-    return (whitened, centroid_means)
+    return factor_and_solve(gram, embeddings, list_sums, list_counts[:, None], total)
 
 
 def solution(mesh):

time: 462 us -> 259 us (0.56); the launches traced: 455 us -> 258 us
  other arithmetic: 194 us -> 2.15 us
  Pallas kernels: 0 us -> 58.2 us
  matrix products: 38.5 us -> 8.27 us
  local copies, waits for them, and re-layouts: 37.2 us -> 9.11 us
  between operations: 20.9 us -> 16.2 us
    another operation x25 -> x0, other arithmetic: 186 us -> none  [the longest x22 125 us: body(): jnp.linalg.cholesky(gram / total + 1e-05 * jnp.eye(width, dtype=jnp.float...]
    pallas_call x0 -> x1, Pallas kernels: none -> 58.2 us  [factor_and_solve(): pl.pallas_call(functools.partial(factor_kernel, float(total)), out_shape=...]
    another operation x32 -> x0, matrix products: 30.2 us -> none  [the longest x22 18.6 us: whiten_rows(): lax.linalg.triangular_solve(factor, values, left_side=False, lower=True,...]
    another operation x50 -> x0, local copies, waits for them, and re-layouts: 24 us -> none
  transfers between devices with their start and end apart: 4 -> 4, of which waited for: 3 -> 3; matrix products, arithmetic and copies ran while one was open for 55% -> 5% of each run, Pallas kernels for 0% -> 0%
where the time goes in v1:
time: 259 us; the launch traced here: 258 us
  waiting for transfers between devices  147 us (57%)
  Pallas kernels  58.2 us (22%)
  between operations  16.2 us (6%)
  starting transfers between devices  10.9 us (4%)
  local copies, waits for them, and re-layouts  9.11 us (4%)
  matrix products  8.27 us (3%)
  blocking collectives  6.07 us (2%)
    psum x1, waiting for transfers between devices, body(): gram = lax.psum(partial_value, ('rows', 'grp'))  127 us
    pallas_call x1, Pallas kernels, factor_and_solve(): pl.pallas_call(functools.partial(factor_kernel, float(total)), out_shape=...  58.2 us
    all_to_all x1, waiting for transfers between devices, body(): lax.all_to_all(outgoing.reshape(owners, capacity, width), 'rows', split_a...  16.6 us
    all_to_all x1, starting transfers between devices, body(): lax.all_to_all(labels.reshape(owners, capacity), 'rows', split_axis=0, co...  7.31 us
    unnamed x1, blocking collectives  6.07 us
  transfers between devices with their start and end apart: 4, of which 3 were waited for; matrix products, arithmetic and copies ran while one was open for 5% of the time, Pallas kernels for 0%

profile of v1, /device:TPU:0, one launch (start us, length us, event | category | flops | bytes accessed | tf_op | source)
XLA Modules:
  0.0 258.4 jit_solution(2452786525838492678)
XLA Ops:
  8.0 0.0 copy-start
  8.0 0.7 and_select_fusion
  8.7 0.1 fusion.4
  8.8 0.2 reduce_window_sum.11
  9.0 0.2 select_reduce_fusion
  9.2 1.0 scatter_custom_fusion
  10.2 0.7 all_to_all.9
  10.8 7.3 %all-to-all-start = ((s32[8,1,32]{2,1,0:T(1,128)}), s32[8,1,32]{2,1,0:T(1,128)S(1)}, u32[]{:S(2)}, u32[]{:S(2)}) async-start(s32[8,1,32]{2,1,0:T(1,128)} %all_to_all.9), calls=%async_computation | async-start | bytes 8192 | tf_op jit(solution)/shard_map/all_to_all | solution.py:153
  18.1 2.4 scatter_custom_fusion.1
  20.5 4.1 %all-to-all-done = s32[8,1,32]{2,1,0:T(1,128)S(1)} async-done(((s32[8,1,32]{2,1,0:T(1,128)}), s32[8,1,32]{2,1,0:T(1,128)S(1)}, u32[]{:S(2)}, u32[]{:S(2)}) %all-to-all-start) | async-done | bytes 1056 | tf_op jit(solution)/shard_map/all_to_all | solution.py:153
  24.6 3.5 %all-to-all-start.1 = ((f32[8,32,768]{2,1,0:T(8,128)}), f32[8,32,768]{2,1,0:T(8,128)S(1)}, u32[]{:S(2)}, u32[]{:S(2)}) async-start(f32[8,32,768]{2,1,0:T(8,128)} %bitcast), calls=%async_computation.1 | async-start | bytes 1572864 | tf_op jit(solution)/shard_map/all_to_all | solution.py:146
  28.1 0.0 all-reduce.3.cloned.1.call-start
  28.2 0.0 copy-done
  28.2 3.5 %fusion.7 = f32[768,768]{1,0:T(8,128)} fusion(f32[128,768]{1,0:T(8,128)S(1)} %copy-done), kind=kOutput, calls=%fused_computation.19 | convolution fusion | flops 905969664 | bytes 2752512 | tf_op jit(solution)/shard_map/dot_general | solution.py:129
  31.7 0.0 all-reduce.3.cloned.1.call-update
  31.7 0.0 reduce-scatter.2.cloned.1.call-start
  31.8 0.5 broadcast.49
  32.3 0.7 reduce.3
  33.0 0.1 eq.33
  33.0 16.6 %all-to-all-done.1 = f32[8,32,768]{2,1,0:T(8,128)S(1)} async-done(((f32[8,32,768]{2,1,0:T(8,128)}), f32[8,32,768]{2,1,0:T(8,128)S(1)}, u32[]{:S(2)}, u32[]{:S(2)}) %all-to-all-start.1) | async-done | bytes 786464 | tf_op jit(solution)/shard_map/all_to_all | solution.py:146
  49.6 4.7 %fusion = f32[2048,768]{1,0:T(8,128)} fusion(f32[256,768]{1,0:T(8,128)S(1)} %bitcast.7, s32[256]{0:T(256)S(1)} %eq.33), kind=kOutput, calls=%fused_computation.4 | convolution fusion | flops 4832362496 | bytes 7078912 | tf_op jit(solution)/shard_map/dot_general | solution.py:160
  54.4 0.0 reduce-scatter.2.cloned.1.call-update
  54.4 0.6 copy-done.3
  55.0 0.6 dynamic-slice
  56.3 0.3 convert_reduce_fusion
  56.6 6.1 %all-reduce = f32[2048]{0:T(1024)S(1)} all-reduce(f32[2048]{0:T(1024)S(1)} %convert_reduce_fusion), channel_id=3, replica_groups=mesh['rows'=8,'grp'=4] {'grp'}, use_global_device_ids=true, to_apply=%region_7.8.clone | all-reduce | flops 2048 | bytes 16384
  62.7 0.1 dynamic-slice.1
  62.8 0.1 copy.6.n_ref
  62.9 126.7 %all-reduce.3.cloned.1.call-done.gram_ref = f32[768,768]{1,0:T(8,128)} async-done(((f32[768,768]{1,0:T(8,128)}), f32[768,768]{1,0:T(8,128)}) %all-reduce.3.cloned.1.call-update) | async-done | bytes 2359312 | tf_op jit(solution)/shard_map/psum | solution.py:135
  189.6 1.7 copy-done.1
  191.3 1.4 copy-done.2
  192.7 58.2 %shard_map.41 = (f32[128,768]{1,0:T(8,128)}, f32[512,768]{1,0:T(8,128)}) custom-call(f32[768,768]{1,0:T(8,128)S(1)} %copy-done.1, f32[128,768]{1,0:T(8,128)S(1)} %copy-done, f32[512,768]{1,0:T(8,128)S(1)} %copy-done.2, f32[512,1]{1,0:T(8,128)S(1)} %copy.6.n_ref), custom_call_target="tpu_custom_call" | custom-call | tf_op jit(solution)/shard_map/pallas_call | solution.py:105
  (5 shorter events, 0.0 us)
Async XLA Ops:
  8.0 20.2 %copy-start = (f32[128,768]{1,0:T(8,128)S(1)}, f32[128,768]{1,0:T(8,128)}, u32[]{:S(2)}) copy-start(f32[128,768]{1,0:T(8,128)} %e_ref.1) | copy-start | bytes 1179652
  10.8 13.7 %all-to-all-start = ((s32[8,1,32]{2,1,0:T(1,128)}), s32[8,1,32]{2,1,0:T(1,128)S(1)}, u32[]{:S(2)}, u32[]{:S(2)}) async-start(s32[8,1,32]{2,1,0:T(1,128)} %all_to_all.9), calls=%async_computation | async-start | bytes 8192 | tf_op jit(solution)/shard_map/all_to_all | solution.py:153
  24.6 25.1 %all-to-all-start.1 = ((f32[8,32,768]{2,1,0:T(8,128)}), f32[8,32,768]{2,1,0:T(8,128)S(1)}, u32[]{:S(2)}, u32[]{:S(2)}) async-start(f32[8,32,768]{2,1,0:T(8,128)} %bitcast), calls=%async_computation.1 | async-start | bytes 1572864 | tf_op jit(solution)/shard_map/all_to_all | solution.py:146
  28.1 161.5 %all-reduce.3.cloned.1.call-start = ((), (), s32[]{:S(2)}) async-start(), calls=%async_computation.3 | async-start | bytes 4718592 | tf_op jit(solution)/shard_map/psum | solution.py:135
  31.7 157.9 %reduce-scatter.2.cloned.1.call-start = ((), (), s32[]{:S(2)}) async-start(), calls=%async_computation.4 | async-start | bytes 7864320 | tf_op jit(solution)/shard_map/reduce_scatter | solution.py:168
  54.4 0.7 copy-start.3
  189.6 1.7 copy-start.1
  191.3 1.4 copy-start.2
Sparse Core Ops, SparseCore 0:
  34.5 155.1 all-reduce.2
Sparse Core Ops, SparseCore 1:
  54.5 57.8 reduce-scatter.1

commit v2 on v1

--- a/solution.py
+++ b/solution.py
@@ -74,12 +74,129 @@
     lax.fori_loop(0, BLOCK // PANEL, step, 0)
 
 
-def factor_kernel(total, gram_ref, e_ref, s_ref, n_ref, w_ref, m_ref, a_ref, x_ref, d_ref, v_ref):
-    width = gram_ref.shape[0]
+def block_pairs(width):
+    blocks = width // BLOCK
+    return [(i, j) for i in range(blocks) for j in range(i, blocks)]
+
+
+def gram_kernel(e_ref, g_ref):
+    width = e_ref.shape[1]
+    used = 0
+    for i in range(width // BLOCK):
+        lo = i * BLOCK
+        strip = dot(e_ref[:, lo : lo + BLOCK], e_ref[:, lo:], ((0,), (0,)))
+        for j in range(strip.shape[1] // BLOCK):
+            g_ref[used : used + BLOCK, :] = strip[:, j * BLOCK : (j + 1) * BLOCK]
+            used += BLOCK
+    if used < g_ref.shape[0]:
+        g_ref[used:, :] = jnp.zeros((g_ref.shape[0] - used, BLOCK), jnp.float32)
+
+
+def local_gram(embeddings, devices):
+    width = embeddings.shape[1]
+    unit = devices * 8
+    rows = len(block_pairs(width)) * BLOCK
+    rows = (rows + unit - 1) // unit * unit
+    vmem = pl.BlockSpec(memory_space=pltpu.VMEM)
+    return pl.pallas_call(
+        gram_kernel,
+        out_shape=jax.ShapeDtypeStruct((rows, BLOCK), jnp.float32),
+        in_specs=[vmem],
+        out_specs=vmem,
+        compiler_params=pltpu.CompilerParams(vmem_limit_bytes=32 * 1024 * 1024),
+    )(embeddings)
+
+
+def reduce_kernel(links, g_ref, out_ref, acc_ref, in_ref, send_sem, recv_sem):
+    partners, bits = [], []
+    for axis, bit in links:
+        me = lax.axis_index(axis)
+        one = lax.rem(me // bit, 2)
+        bits.append(one)
+        partners.append({axis: me + bit - 2 * bit * one})
+    barrier = pltpu.get_barrier_semaphore()
+    for partner in partners:
+        pl.semaphore_signal(
+            barrier, inc=1, device_id=partner, device_id_type=pl.DeviceIdType.MESH
+        )
+    pl.semaphore_wait(barrier, len(partners))
+    steps = len(links)
+    size = g_ref.shape[0]
+    start = 0
+    starts = []
+    landed = 0
+    for k in range(steps):
+        half = size // 2
+        source = g_ref if k == 0 else acc_ref
+        keep = pl.multiple_of(start + bits[k] * half, 8)
+        give = pl.multiple_of(start + (1 - bits[k]) * half, 8)
+        copy = pltpu.make_async_remote_copy(
+            src_ref=source.at[pl.ds(give, half)],
+            dst_ref=in_ref.at[pl.ds(landed, half)],
+            send_sem=send_sem.at[k],
+            recv_sem=recv_sem.at[k],
+            device_id=partners[k],
+            device_id_type=pl.DeviceIdType.MESH,
+        )
+        copy.start()
+        copy.wait()
+        total = source[pl.ds(keep, half), :] + in_ref[pl.ds(landed, half), :]
+        if k == steps - 1:
+            out_ref[pl.ds(keep, half), :] = total
+        else:
+            acc_ref[pl.ds(keep, half), :] = total
+        landed += half
+        start, size = keep, half
+        starts.append(keep)
+    for k in reversed(range(steps)):
+        here = pl.ds(starts[k], size)
+        copy = pltpu.make_async_remote_copy(
+            src_ref=out_ref.at[here],
+            dst_ref=out_ref.at[here],
+            send_sem=send_sem.at[steps + k],
+            recv_sem=recv_sem.at[steps + k],
+            device_id=partners[k],
+            device_id_type=pl.DeviceIdType.MESH,
+        )
+        copy.start()
+        copy.wait()
+        size *= 2
+
+
+def reduce_everywhere(packed):
+    links = []
+    for axis in ("grp", "rows"):
+        bit = 1
+        while bit < lax.axis_size(axis):
+            links.append((axis, bit))
+            bit *= 2
+    vmem = pl.BlockSpec(memory_space=pltpu.VMEM)
+    return pl.pallas_call(
+        functools.partial(reduce_kernel, links),
+        out_shape=jax.ShapeDtypeStruct(packed.shape, jnp.float32),
+        in_specs=[vmem],
+        out_specs=vmem,
+        scratch_shapes=[
+            pltpu.VMEM(packed.shape, jnp.float32),
+            pltpu.VMEM(packed.shape, jnp.float32),
+            pltpu.SemaphoreType.DMA((2 * len(links),)),
+            pltpu.SemaphoreType.DMA((2 * len(links),)),
+        ],
+        compiler_params=pltpu.CompilerParams(
+            collective_id=0, has_side_effects=True, vmem_limit_bytes=24 * 1024 * 1024
+        ),
+    )(packed)
+
+
+def factor_kernel(total, g_ref, e_ref, w_ref, x_ref, a_ref, d_ref, v_ref):
+    width = x_ref.shape[0]
     r = lax.broadcasted_iota(jnp.int32, (BLOCK, BLOCK), 0)
     c = lax.broadcasted_iota(jnp.int32, (BLOCK, BLOCK), 1)
     eye = jnp.where(r == c, 1.0, 0.0).astype(jnp.float32)
-    a_ref[...] = gram_ref[...] / total
+    for n, (i, j) in enumerate(block_pairs(width)):
+        a_ref[i * BLOCK : (i + 1) * BLOCK, j * BLOCK : (j + 1) * BLOCK] = (
+            g_ref[n * BLOCK : (n + 1) * BLOCK, :] / total
+        )
     x_ref[...] = jnp.zeros_like(x_ref)
     for lo in range(0, width, BLOCK):
         hi = lo + BLOCK
@@ -93,31 +210,68 @@
             x_ref[here, :lo] = dot(inv, x_ref[here, :lo], ((1,), (0,)))
         if hi < width:
             upper = dot(inv, a_ref[here, hi:], ((1,), (0,)))
-            a_ref[hi:, hi:] = a_ref[hi:, hi:] - dot(upper, upper, ((0,), (0,)))
+            for row in range(hi, width, BLOCK):
+                strip = slice(row, row + BLOCK)
+                a_ref[strip, row:] = a_ref[strip, row:] - dot(
+                    upper[:, row - hi : row - hi + BLOCK], upper[:, row - hi :], ((0,), (0,))
+                )
             x_ref[hi:, :hi] = x_ref[hi:, :hi] - dot(upper, x_ref[here, :hi], ((0,), (0,)))
     w_ref[...] = dot(e_ref[...], x_ref[...], ((1,), (1,)))
-    m_ref[...] = dot(s_ref[...], x_ref[...], ((1,), (1,))) / jnp.maximum(n_ref[...], 1.0)
-
-
-def factor_and_solve(gram, embeddings, sums, counts, total):
-    width = gram.shape[0]
+
+
+def factor_and_whiten(packed, embeddings, total):
+    width = embeddings.shape[1]
     vmem = pl.BlockSpec(memory_space=pltpu.VMEM)
     return pl.pallas_call(
         functools.partial(factor_kernel, float(total)),
         out_shape=(
             jax.ShapeDtypeStruct(embeddings.shape, jnp.float32),
-            jax.ShapeDtypeStruct(sums.shape, jnp.float32),
+            jax.ShapeDtypeStruct((width, width), jnp.float32),
         ),
-        in_specs=[vmem] * 4,
+        in_specs=[vmem] * 2,
         out_specs=(vmem, vmem),
         scratch_shapes=[
-            pltpu.VMEM((width, width), jnp.float32),
             pltpu.VMEM((width, width), jnp.float32),
             pltpu.VMEM((BLOCK, 2 * BLOCK), jnp.float32),
             pltpu.VMEM((BLOCK, BLOCK), jnp.float32),
         ],
+        cost_estimate=pl.CostEstimate(
+            flops=12 * width**3, bytes_accessed=12 * width**2, transcendentals=width
+        ),
+        compiler_params=pltpu.CompilerParams(vmem_limit_bytes=32 * 1024 * 1024),
+    )(packed, embeddings)
+
+
+def means_kernel(rows_ref, tags_ref, x_ref, m_ref):
+    lists, width = m_ref.shape
+    count = rows_ref.shape[0]
+    index = lax.broadcasted_iota(jnp.int32, (lists, count), 0)
+    base = lax.axis_index("grp") * lists
+    hit = tags_ref[...].astype(jnp.int32) == index + (base + 1)
+    member = jnp.where(hit, 1.0, 0.0).astype(jnp.float32)
+    counts = jnp.sum(member, axis=1, keepdims=True)
+    member = member.astype(jnp.bfloat16)
+    sums = jnp.zeros((lists, width), jnp.float32)
+    for part in split3(rows_ref[...]):
+        sums = sums + lax.dot_general(
+            member,
+            part.astype(jnp.bfloat16),
+            (((1,), (0,)), ((), ())),
+            preferred_element_type=jnp.float32,
+        )
+    m_ref[...] = dot(sums, x_ref[...], ((1,), (1,))) / jnp.maximum(counts, 1.0)
+
+
+def centroid_means_of(rows, tags, inverse, lists):
+    width = inverse.shape[0]
+    vmem = pl.BlockSpec(memory_space=pltpu.VMEM)
+    return pl.pallas_call(
+        means_kernel,
+        out_shape=jax.ShapeDtypeStruct((lists, width), jnp.float32),
+        in_specs=[vmem] * 3,
+        out_specs=vmem,
         compiler_params=pltpu.CompilerParams(vmem_limit_bytes=48 * 1024 * 1024),
-    )(gram, embeddings, sums, counts)
+    )(rows, tags, inverse)
 
 
 def body(embeddings, assignments):
@@ -126,13 +280,9 @@
     owners = lax.axis_size("rows")
     groups = lax.axis_size("grp")
     total = rows_here * owners * groups
-    partial_value = jnp.dot(
-        embeddings.T,
-        embeddings,
-        precision=lax.Precision.HIGHEST,
-        preferred_element_type=jnp.float32,
-    )
-    gram = lax.psum(partial_value, ("rows", "grp"))
+    gram = reduce_everywhere(local_gram(embeddings, owners * groups))
+    whitened, inverse = factor_and_whiten(gram, embeddings, total)
+
     per_owner = CENTROIDS // owners
     capacity = max(2, 2 * rows_here // owners)
     target = assignments // per_owner
@@ -140,35 +290,26 @@
     hits = (target[:, None] == jnp.arange(owners, dtype=jnp.int32)[None, :]).astype(jnp.int32)
     rank = jnp.sum(hits * (jnp.cumsum(hits, axis=0) - 1), axis=1)
     slot = target * capacity + rank
-    outgoing = jnp.zeros((owners * capacity, width), jnp.float32).at[slot].set(embeddings)
-    labels = jnp.full((owners * capacity,), -1, jnp.int32).at[slot].set(local)
-    incoming, tags = (
-        lax.all_to_all(
-            outgoing.reshape(owners, capacity, width),
-            "rows",
-            split_axis=0,
-            concat_axis=0,
-            tiled=True,
-        ),
-        lax.all_to_all(
-            labels.reshape(owners, capacity), "rows", split_axis=0, concat_axis=0, tiled=True
-        ),
-    )
-    member = (tags.reshape(-1)[None, :] == jnp.arange(per_owner, dtype=jnp.int32)[:, None]).astype(
-        jnp.float32
-    )
-    list_sums = jnp.dot(
-        member,
-        incoming.reshape(-1, width),
-        precision=lax.Precision.HIGHEST,
-        preferred_element_type=jnp.float32,
-    )
-    list_counts = jnp.sum(member, axis=1)
-    list_sums, list_counts = (
-        lax.psum_scatter(list_sums, "grp", scatter_dimension=0, tiled=True),
-        lax.psum_scatter(list_counts, "grp", scatter_dimension=0, tiled=True),
-    )
-    return factor_and_solve(gram, embeddings, list_sums, list_counts[:, None], total)
+    tagged = jnp.concatenate(
+        [
+            embeddings,
+            jnp.broadcast_to((local + 1).astype(jnp.float32)[:, None], (rows_here, BLOCK)),
+        ],
+        axis=1,
+    )
+    outgoing = jnp.zeros((owners * capacity, width + BLOCK), jnp.float32).at[slot].set(tagged)
+    incoming = lax.all_to_all(
+        outgoing.reshape(owners, capacity, width + BLOCK),
+        "rows",
+        split_axis=0,
+        concat_axis=0,
+        tiled=True,
+    )
+    incoming = lax.all_gather(incoming.reshape(-1, width + BLOCK), "grp", axis=0, tiled=True)
+    means = centroid_means_of(
+        incoming[:, :width], incoming[:, width][None, :], inverse, per_owner // groups
+    )
+    return (whitened, means)
 
 
 def solution(mesh):

time: 259 us -> 167 us (0.64)
  waiting for transfers between devices: 147 us -> 0.02 us
  Pallas kernels: 58.2 us -> 116 us
  blocking collectives: 6.07 us -> 30.5 us
  starting transfers between devices: 10.9 us -> 0.04 us
  matrix products: 8.27 us -> 0 us
  local copies, waits for them, and re-layouts: 9.11 us -> 3.42 us
    psum x1 -> x0, waiting for transfers between devices: 127 us -> none  [body(): gram = lax.psum(partial_value, ('rows', 'grp'))]
    pallas_call x1 -> x4, Pallas kernels: 58.2 us -> 116 us  [the longest x1 52.7 us: factor_and_whiten(): pl.pallas_call(functools.partial(factor_kernel, float(total)), out_shape=...]
    all_to_all x0 -> x1, blocking collectives: none -> 30.5 us  [body(): lax.all_to_all(outgoing.reshape(owners, capacity, width + BLOCK), 'rows',...]
    all_to_all x2 -> x0, waiting for transfers between devices: 20.7 us -> none  [the longest x1 16.6 us: body(): lax.all_to_all(outgoing.reshape(owners, capacity, width), 'rows', split_a...]
    all_to_all x2 -> x0, starting transfers between devices: 10.9 us -> none  [the longest x1 7.31 us: body(): lax.all_to_all(labels.reshape(owners, capacity), 'rows', split_axis=0, co...]
    dot_general x2 -> x0, matrix products: 8.27 us -> none  [the longest x1 4.74 us: body(): jnp.dot(member, incoming.reshape(-1, width), precision=lax.Precision.HIGH...]
    unnamed x1 -> x0, blocking collectives: 6.07 us -> none
    unnamed x10 -> x2, local copies, waits for them, and re-layouts: 4.37 us -> 0.01 us
  transfers between devices with their start and end apart: 4 -> 1, of which waited for: 3 -> 0; matrix products, arithmetic and copies ran while one was open for 5% -> 0% of each run, Pallas kernels for 0% -> 64%
where the time goes in v2:
time: 167 us
  Pallas kernels  116 us (69%)
  blocking collectives  30.5 us (18%)
  between operations  14.1 us (8%)
  local copies, waits for them, and re-layouts  3.42 us (2%)
  other arithmetic  2.88 us (2%)
    pallas_call x1, Pallas kernels, factor_and_whiten(): pl.pallas_call(functools.partial(factor_kernel, float(total)), out_shape=...  52.7 us
    pallas_call x1, Pallas kernels, reduce_everywhere(): pl.pallas_call(functools.partial(reduce_kernel, links), out_shape=jax.Sha...  52.4 us
    all_to_all x1, blocking collectives, body(): lax.all_to_all(outgoing.reshape(owners, capacity, width + BLOCK), 'rows',...  30.5 us
    pallas_call x1, Pallas kernels, centroid_means_of(): pl.pallas_call(means_kernel, out_shape=jax.ShapeDtypeStruct((lists, width...  9.39 us
  transfers between devices with their start and end apart: 1, of which 0 were waited for; matrix products, arithmetic and copies ran while one was open for 0% of the time, Pallas kernels for 64%

profile of v2, /device:TPU:0, one launch (start us, length us, event | category | flops | bytes accessed | tf_op | source)
XLA Modules:
  0.0 166.8 jit_solution(15582554146828584567)
XLA Ops:
  7.2 0.0 copy-start
  7.2 0.0 all-gather.2.cloned.1.call-start
  7.2 0.7 fusion.7
  7.9 0.1 fusion.5
  8.0 0.2 reduce_window_sum.11
  8.2 0.2 select_reduce_fusion
  8.4 0.1 broadcast_in_dim.16
  8.5 1.7 %scatter_custom_fusion = f32[256,896]{1,0:T(8,128)S(1)} fusion(s32[128]{0:T(128)S(1)} %compare_select_fusion, f32[128,128]{1,0:T(8,128)S(1)} %broadcast_in_dim.16, f32[]{:T(128)} %constant.44, f32[128,768]{1,0:T(8,128)} %e_ref.3, f32[]{:T(128)} %constant.34.clone.1), kind=kCustom, calls=%fused_computation.2 | custom fusion | flops 114688 | bytes 1376264 | tf_op jit(solution)/shard_map/scatter | solution.py:300
  10.2 30.5 %all_to_all.5 = f32[8,32,896]{2,1,0:T(8,128)} all-to-all(f32[8,32,896]{2,1,0:T(8,128)S(1)} %bitcast.6), channel_id=1, replica_groups=mesh['rows'=8,'grp'=4] {'rows'}, dimensions={0} | all-to-all | bytes 1835008 | tf_op jit(solution)/shard_map/all_to_all | solution.py:301
  40.7 0.0 all-gather.2.cloned.1.call-update
  40.7 0.0 copy-done
  40.7 1.3 shard_map.41.g_ref
  42.0 52.4 %shard_map.42.g_ref = f32[2816,128]{1,0:T(8,128)S(1)} custom-call(f32[2816,128]{1,0:T(8,128)S(1)} %shard_map.41.g_ref), custom_call_target="tpu_custom_call" | custom-call | tf_op jit(solution)/shard_map/pallas_call | solution.py:174
  94.5 52.7 %shard_map.43 = (f32[128,768]{1,0:T(8,128)}, f32[768,768]{1,0:T(8,128)S(1)}) custom-call(f32[2816,128]{1,0:T(8,128)S(1)} %shard_map.42.g_ref, f32[128,768]{1,0:T(8,128)S(1)} %copy-done), custom_call_target="tpu_custom_call" | custom-call | flops 5435817984 | bytes 7077888 | tf_op jit(solution)/shard_map/pallas_call | solution.py:225
  147.2 0.0 all-gather.2.cloned.1.call-done
  147.2 1.2 slice_reduce_fusion
  148.5 2.1 %slice.8.rows_ref = f32[1024,768]{1,0:T(8,128)S(1)} slice(f32[1024,896]{1,0:T(8,128)} %all-gather.2.cloned.1.call-done), slice={[0:1024], [0:768]} | slice | bytes 6291456 | tf_op jit(solution)/shard_map/slice | solution.py:310
  150.6 9.4 %shard_map.44 = f32[512,768]{1,0:T(8,128)} custom-call(f32[1024,768]{1,0:T(8,128)S(1)} %slice.8.rows_ref, f32[1,1024]{1,0:T(1,128)S(1)} %bitcast.4, f32[768,768]{1,0:T(8,128)S(1)} %get-tuple-element.5.x_ref), custom_call_target="tpu_custom_call" | custom-call | tf_op jit(solution)/shard_map/pallas_call | solution.py:268
  (1 shorter events, 0.0 us)
Async XLA Ops:
  7.2 33.6 %copy-start = (f32[128,768]{1,0:T(8,128)S(1)}, f32[128,768]{1,0:T(8,128)}, u32[]{:S(2)}) copy-start(f32[128,768]{1,0:T(8,128)} %e_ref.3) | copy-start | bytes 1179652
  7.2 140.1 %all-gather.2.cloned.1.call-start = ((), (), s32[]{:S(2)}) async-start(), calls=%async_computation.1 | async-start | bytes 4587520 | tf_op jit(solution)/shard_map/all_gather | solution.py:308
Sparse Core Ops, SparseCore 0:
  40.8 35.8 all-gather.1
